TPU v7x, 32 devices: a whole 2x2x4 slice. The times are simulated.
32 devices in a mesh: clips: 2 (over y), tiles: 16 (over z, x, core).
Axes of the slice: x: 2, y: 2, z: 4, core: 2. Of those that a mesh axis runs over, the one named last changes fastest.
Arguments:
- frames: bfloat16 [4, 64, 256, 128], P(None, None, ('clips', 'tiles')), parts along dimension 2, may hold values from -6 to 6
- motion_forward: int32 [3, 512], P(None, ('clips', 'tiles')), parts along dimension 1, may hold values from 0 to 255, as said below
- motion_backward: int32 [3, 512], P(None, ('clips', 'tiles')), parts along dimension 1, may hold values from 0 to 255, as said below
- join_weight: bfloat16 [2, 64, 128], replicated, may hold values from -0.5 to 0.5
- conv_weight: bfloat16 [2, 4, 9, 64, 64], replicated, may hold values from -0.125 to 0.125
Outputs:
- forward_features: bfloat16 [4, 64, 256, 128], P(None, None, ('clips', 'tiles')), parts along dimension 2
- backward_features: bfloat16 [4, 64, 256, 128], P(None, None, ('clips', 'tiles')), parts along dimension 2
There are 2 independent parts, one for each index of `clips`. A program takes and returns all parts, laid end to end along the dimension named above; an argument that names none is the same for every part. Nothing has to cross between parts.
Inputs may be any that keep to these rules, and one draw needn't show every extreme that they name: `motion_forward`: entries are block numbers of the frame; block number k lies in rows held by device k // 16. A block of device d takes a block of a device at most 2 away from d, at most two block columns to either side of its own column. Of the 16 blocks of one device, either none or exactly 4 take blocks of any one other device; in every frame some device takes 4 blocks from each device up to 2 away on both sides. `motion_backward`: entries are block numbers of the frame; block number k lies in rows held by device k // 16. A block of device d takes a block of a device at most 2 away from d, at most two block columns to either side of its own column. Of the 16 blocks of one device, either none or exactly 4 take blocks of any one other device; in every frame some device takes 4 blocks from each device up to 2 away on both sides.
All inputs are finite; a program needn't handle non-finite values.
Results may differ from a plain program's by a relative error of at most 0.018.
Values may be sent and summed in bfloat16 or wider, within the bound.
A program may use at most 64 MiB of HBM per device.

v0:
```python
import functools

import jax
import jax.numpy as jnp
from jax import lax
from jax.experimental import pallas as pl
from jax.experimental.pallas import tpu as pltpu
from jax.sharding import PartitionSpec as P

BS = 8
REACH = 2
OFFSETS = tuple(o for o in range(-REACH, REACH + 1) if o != 0)


def leaky(value):
    return jnp.where(value >= 0, value, 0.1 * value)


def blockdiag(tile):
    blank = jnp.zeros(tile.shape, tile.dtype)
    return jnp.concatenate(
        [jnp.concatenate([tile, blank], axis=1), jnp.concatenate([blank, tile], axis=1)], axis=0
    )


def matmul_t(left, right):
    return lax.dot_general(
        left, right, (((1,), (1,)), ((), ())), preferred_element_type=jnp.float32
    )


def sweep_kernel(
    dims,
    frames_ref,
    mf_ref,
    mb_ref,
    join_ref,
    conv_ref,
    ahead_ref,
    behind_ref,
    x_ref,
    flip,
    wj_ref,
    wc_ref,
    mine,
    theirs,
    table_v,
    table_s,
    cand,
    packed,
    landed,
    aligned,
    h_ref,
    z_ref,
    edge_out,
    edge_in,
    m_send,
    m_recv,
    f_send,
    f_recv,
    e_send,
    e_recv,
    t_sem,
):
    frame_count, rows, cols, channels, layers, devices = dims
    outs = (ahead_ref, behind_ref)
    lanes = 2 * channels
    width = cols // 2
    bc = cols // BS
    pairs = bc // 2
    cap = bc // (2 * REACH)
    sides = len(OFFSETS)
    kept = pairs + sides * cap // 2
    cell = BS * BS
    own = rows * width
    halo = layers * width
    me = lax.axis_index("tiles")

    def present(offset):
        return (me + offset >= 0) & (me + offset < devices)

    def remote(source, target, send, receive, offset):
        return pltpu.make_async_remote_copy(
            src_ref=source,
            dst_ref=target,
            send_sem=send,
            recv_sem=receive,
            device_id={"tiles": me + offset},
            device_id_type=pl.DeviceIdType.MESH,
        )

    def motion_copy(oi, slot):
        return remote(mine, theirs.at[slot], m_send.at[oi], m_recv.at[slot], OFFSETS[oi])

    def feature_copy(d, step, oi, slot):
        return remote(
            packed.at[d, step, oi], landed.at[d, step, slot],
            f_send.at[d, step, oi], f_recv.at[d, step, slot], OFFSETS[oi],
        )

    def edge_copy(d, step, side, slot):
        return remote(
            edge_out.at[d, step, side], edge_in.at[d, step, slot],
            e_send.at[d, step, side], e_recv.at[d, step, slot], 1 if side else -1,
        )

    barrier = pltpu.get_barrier_semaphore()
    for offset in OFFSETS:
        @pl.when(present(offset))
        def _():
            pl.semaphore_signal(
                barrier, inc=1, device_id={"tiles": me + offset},
                device_id_type=pl.DeviceIdType.MESH,
            )

    mine[...] = jnp.zeros(mine.shape, jnp.int32)
    for step in range(frame_count - 1):
        mine[step:step + 1, 0:bc] = mf_ref[step:step + 1, :]
        back = frame_count - 2 - step
        mine[frame_count - 1 + step:frame_count + step, 0:bc] = mb_ref[back:back + 1, :]

    identity = (
        lax.broadcasted_iota(jnp.int32, (channels, channels), 0)
        == lax.broadcasted_iota(jnp.int32, (channels, channels), 1)
    ).astype(jnp.bfloat16)
    for d in range(2):
        joined = join_ref[d]
        wj_ref[d, :, :lanes] = blockdiag(joined[:, :channels])
        wj_ref[d, :, lanes:] = blockdiag(joined[:, channels:])

        def build_layer(layer, carry):
            stacked = conv_ref[d, layer].reshape(9 * channels, channels)
            turned = matmul_t(identity, stacked).astype(jnp.bfloat16)
            blank = jnp.zeros((channels, channels), jnp.bfloat16)

            def tap(down, across):
                start = (3 * down + across) * channels
                return turned[:, start:start + channels]

            for side in range(2):
                order = (0, 1, 2, None) if side == 0 else (1, 0, None, 2)
                depth = (0, 1, 2, None) if side == 0 else (0, 1, None, 2)
                for k, down in enumerate(depth):
                    wc_ref[d, layer, side, k * channels:(k + 1) * channels, :] = jnp.concatenate(
                        [
                            blank if down is None or across is None else tap(down, across)
                            for across in order
                        ],
                        axis=1,
                    )
            return carry

        lax.fori_loop(0, layers, build_layer, 0)

    def picker(count):
        row = lax.broadcasted_iota(jnp.int32, (count, 2 * count), 0)
        column = lax.broadcasted_iota(jnp.int32, (count, 2 * count), 1)
        return ((column == row) | (column == row + count)).astype(jnp.bfloat16)

    def load_frame(f, carry):
        flip[0] = frames_ref[f].astype(jnp.float32).reshape(channels * rows, cols)
        first = lax.broadcasted_iota(jnp.int32, (channels, cols), 1) < width
        parts = []
        for r in range(rows):
            row = flip[0, pl.ds(r, channels, stride=rows), :]
            parts += [jnp.where(first, row, 0.0), jnp.where(first, 0.0, row)]
        moved = matmul_t(picker(width), jnp.concatenate(parts, axis=0).astype(jnp.bfloat16))
        for r in range(rows):
            x_ref[f, r * width:(r + 1) * width, :] = moved[:, r * lanes:(r + 1) * lanes].astype(
                jnp.bfloat16
            )
        return carry

    lax.fori_loop(0, frame_count, load_frame, 0)

    def emit(d, t):
        value = h_ref[d, halo:halo + own, :].astype(jnp.float32).reshape(rows, width, lanes)
        first = lax.broadcasted_iota(jnp.int32, value.shape, 2) < channels
        split = jnp.concatenate(
            [jnp.where(first, value, 0.0), jnp.where(first, 0.0, value)], axis=1
        ).reshape(rows * cols, lanes).astype(jnp.bfloat16)
        moved = matmul_t(picker(channels), split)
        for r in range(rows):
            flip[d, pl.ds(r, channels, stride=rows), :] = moved[:, r * cols:(r + 1) * cols]
        now = t if d == 0 else frame_count - 1 - t
        outs[d][now] = flip[d].reshape(channels, rows, cols).astype(jnp.bfloat16)

    peers = jnp.minimum(me, REACH) + jnp.minimum(devices - 1 - me, REACH)
    pl.semaphore_wait(barrier, peers)

    for oi, offset in enumerate(OFFSETS):
        @pl.when(present(offset))
        def _():
            motion_copy(oi, sides - 1 - oi).start()

    lane = lax.broadcasted_iota(jnp.int32, mine.shape, 1)

    def prefix(flags):
        total = flags
        shift = 1
        while shift < bc:
            total = total + jnp.where(lane >= shift, pltpu.roll(total, shift, axis=1), 0)
            shift *= 2
        return total - flags

    def owned(motion, device):
        low = device * bc
        return (motion >= low) & (motion < low + bc) & (lane < bc)

    def own_code(local):
        return jnp.where(local < pairs, local, kept + local - pairs)

    def swapped(code):
        return jnp.where(code >= kept, code - kept, code + kept)

    def build_tables():
        motion = mine[...]
        picks = jnp.where(owned(motion, me), own_code(motion - me * bc), 0)
        for oi, offset in enumerate(OFFSETS):
            match = owned(motion, me + offset)
            rank = jnp.minimum(prefix(match.astype(jnp.int32)), cap - 1)
            base = pairs + oi * cap // 2
            code = jnp.where(rank < cap // 2, base + rank, kept + base + rank - cap // 2)
            picks = picks + jnp.where(match, code, 0)
        table_v[sides] = jnp.where(lane < pairs, picks, swapped(picks))
        for oi, offset in enumerate(OFFSETS):
            @pl.when(present(offset))
            def _():
                motion_copy(oi, oi).wait_send()
                motion_copy(oi, oi).wait_recv()
                wanted = theirs[oi]
                match = owned(wanted, me)
                rank = prefix(match.astype(jnp.int32))
                code = own_code(wanted - me * bc)
                gathered = jnp.zeros(mine.shape, jnp.int32)
                for slot in range(cap):
                    held = code if slot < cap // 2 else swapped(code)
                    value = jnp.where(match & (rank == slot), held, 0)
                    shift = 1
                    while shift < bc:
                        value = value + pltpu.roll(value, shift, axis=1)
                        shift *= 2
                    value = pltpu.roll(value, 1 + slot, axis=1)
                    gathered = jnp.where(lane == bc + slot, value, gathered)
                table_v[oi] = gathered

            @pl.when(jnp.logical_not(present(offset)))
            def _():
                table_v[oi] = jnp.zeros(mine.shape, jnp.int32)
        load = pltpu.make_async_copy(table_v, table_s, t_sem)
        load.start()
        load.wait()

    left_half = lax.broadcasted_iota(jnp.int32, (rows, BS, lanes), 2) < channels

    def keep(d, index, tile):
        cand[d, index] = tile
        cand[d, kept + index] = pltpu.roll(tile, channels, axis=2)

    def activate(d, slot, start, value):
        size = value.shape[0]
        z_ref[d, slot, 0, start:start + size, :] = value.astype(jnp.bfloat16)
        z_ref[d, slot, 1, start:start + size, :] = pltpu.roll(value, channels, axis=1).astype(
            jnp.bfloat16
        )

    def begin(d, t):
        @pl.when(t == 0)
        def _():
            aligned[d] = jnp.zeros(aligned.shape[1:], aligned.dtype)

        @pl.when(t > 0)
        def _():
            step = t - 1
            row = d * (frame_count - 1) + step
            for oi, offset in enumerate(OFFSETS):
                @pl.when(present(offset))
                def _():
                    feature_copy(d, step, oi, oi).wait_recv()
                    tiles = landed[d, step, oi].astype(jnp.float32)
                    tiles = tiles.reshape(cap // 2, BS, BS, lanes)
                    for pair in range(cap // 2):
                        keep(d, pairs + oi * cap // 2 + pair, tiles[pair])
            for j in range(pairs):
                low = table_s[sides, row, j]
                high = table_s[sides, row, pairs + j]
                aligned[d, :, j * BS:(j + 1) * BS, :] = jnp.where(
                    left_half, cand[d, low], cand[d, high]
                )

        now = t if d == 0 else frame_count - 1 - t
        both = jnp.concatenate(
            [aligned[d].reshape(own, lanes).astype(jnp.bfloat16), x_ref[now]], axis=1
        )
        first = matmul_t(both, wj_ref[d]).astype(jnp.bfloat16)
        edge_out[d, t, 0] = first[:halo]
        edge_out[d, t, 1] = first[own - halo:]
        for side in range(2):
            @pl.when(present(1 if side else -1))
            def _():
                edge_copy(d, t, side, 1 - side).start()
        h_ref[d, halo:halo + own, :] = first
        activate(d, 0, halo, leaky(first.astype(jnp.float32)))

    top_inside = (me > 0).astype(jnp.float32)
    bottom_inside = (me < devices - 1).astype(jnp.float32)

    def finish(d, t):
        for side in range(2):
            start = side * (halo + own)

            @pl.when(present(1 if side else -1))
            def _():
                edge_copy(d, t, side, side).wait_recv()
                edge = edge_in[d, t, side]
                h_ref[d, start:start + halo, :] = edge
                activate(d, 0, start, leaky(edge.astype(jnp.float32)))

            @pl.when(jnp.logical_not(present(1 if side else -1)))
            def _():
                h_ref[d, start:start + halo, :] = jnp.zeros((halo, lanes), jnp.bfloat16)
                for swap in range(2):
                    z_ref[d, 0, swap, start:start + halo, :] = jnp.zeros(
                        (halo, lanes), jnp.bfloat16
                    )

        for layer in range(layers):
            out_rows = rows + 2 * (layers - 1 - layer)
            size = out_rows * width
            plain = z_ref.at[d, layer % 2, 0]
            turned = z_ref.at[d, layer % 2, 1]
            rows0 = pl.ds(layer * width, size)
            rows1 = pl.ds((layer + 1) * width, size)
            below = plain[(layer + 2) * width:(layer + 2) * width + size, :]
            low = lax.broadcasted_iota(jnp.int32, (size, lanes), 1) < channels
            upper = jnp.where(low, plain[rows0, :], turned[rows1, :])
            lower = jnp.where(low, turned[rows0, :], plain[rows1, :])
            one = jnp.dot(
                jnp.concatenate([upper, below], axis=1), wc_ref[d, layer, 0],
                preferred_element_type=jnp.float32,
            )
            two = jnp.dot(
                jnp.concatenate([lower, below], axis=1), wc_ref[d, layer, 1],
                preferred_element_type=jnp.float32,
            )
            tap0 = jnp.where(low, one[:, :lanes], two[:, :lanes])
            tap1 = pltpu.roll(jnp.where(low, two[:, :lanes], one[:, :lanes]), channels, axis=1)
            tap2 = jnp.where(low, one[:, lanes:], two[:, lanes:])
            place = lax.broadcasted_iota(jnp.int32, (out_rows, BS, lanes), 1)
            lefts = lax.broadcasted_iota(jnp.int32, (out_rows, BS, lanes), 2) < channels
            before = pltpu.roll(tap0.reshape(out_rows, width, lanes), 1, axis=1)
            seam = before[:, :BS]
            crossed = jnp.where(lefts, 0.0, pltpu.roll(seam, channels, axis=2))
            before = jnp.concatenate(
                [jnp.where(place == 0, crossed, seam), before[:, BS:]], axis=1
            ).reshape(size, lanes)
            after = pltpu.roll(tap2.reshape(out_rows, width, lanes), width - 1, axis=1)
            seam = after[:, width - BS:]
            crossed = jnp.where(lefts, pltpu.roll(seam, channels, axis=2), 0.0)
            after = jnp.concatenate(
                [after[:, :width - BS], jnp.where(place == BS - 1, crossed, seam)], axis=1
            ).reshape(size, lanes)
            base = (layer + 1) * width
            total = h_ref[d, base:base + size, :].astype(jnp.float32) + tap1
            rounded = (total + before + after).astype(jnp.bfloat16)
            if layer < layers - 1:
                h_ref[d, base:base + size, :] = rounded
                active = leaky(rounded.astype(jnp.float32))
                outside = halo - base
                active = jnp.concatenate(
                    [
                        active[:outside] * top_inside,
                        active[outside:size - outside],
                        active[size - outside:] * bottom_inside,
                    ],
                    axis=0,
                )
                activate(d, 1 - layer % 2, base, active)
            else:
                grid = rounded.astype(jnp.float32).reshape(rows, pairs, BS, lanes)
                for j in range(pairs):
                    keep(d, j, grid[:, j])
                h_ref[d, base:base + size, :] = rounded

        @pl.when(t < frame_count - 1)
        def _():
            row = d * (frame_count - 1) + t
            for oi, offset in enumerate(OFFSETS):
                @pl.when(present(offset))
                def _():
                    for pair in range(cap // 2):
                        low = table_s[oi, row, bc + pair]
                        high = table_s[oi, row, bc + cap // 2 + pair]
                        block = jnp.where(left_half, cand[d, low], cand[d, high])
                        packed[d, t, oi, pair * cell:(pair + 1) * cell, :] = block.reshape(
                            cell, lanes
                        ).astype(jnp.bfloat16)
                    feature_copy(d, t, oi, sides - 1 - oi).start()

    def frame_step(t, carry):
        begin(0, t)
        begin(1, t)

        @pl.when(t == 0)
        def _():
            build_tables()

        finish(0, t)
        finish(1, t)
        emit(0, t)
        emit(1, t)
        return carry

    lax.fori_loop(0, frame_count, frame_step, 0)

    for d in range(2):
        for step in range(frame_count):
            for side in range(2):
                @pl.when(present(1 if side else -1))
                def _():
                    edge_copy(d, step, side, side).wait_send()
            if step < frame_count - 1:
                for oi, offset in enumerate(OFFSETS):
                    @pl.when(present(offset))
                    def _():
                        feature_copy(d, step, oi, oi).wait_send()


def on_device(frames, motion_forward, motion_backward, join_weight, conv_weight):
    frame_count, channels, rows, cols = frames.shape
    layers = conv_weight.shape[1]
    devices = lax.axis_size("tiles")
    lanes = 2 * channels
    width = cols // 2
    own = rows * width
    halo = layers * width
    bc = rows // BS * (cols // BS)
    cap = bc // (2 * REACH)
    sides = len(OFFSETS)
    steps = frame_count - 1
    kept = bc // 2 + sides * cap // 2

    dims = (frame_count, rows, cols, channels, layers, devices)
    vmem = pl.BlockSpec(memory_space=pltpu.VMEM)
    result = jax.ShapeDtypeStruct(frames.shape, jnp.bfloat16)
    return pl.pallas_call(
        functools.partial(sweep_kernel, dims),
        out_shape=(result, result),
        in_specs=[vmem] * 5,
        out_specs=(vmem, vmem),
        scratch_shapes=[
            pltpu.VMEM((frame_count, own, lanes), jnp.bfloat16),
            pltpu.VMEM((2, channels * rows, cols), jnp.float32),
            pltpu.VMEM((2, lanes, 2 * lanes), jnp.bfloat16),
            pltpu.VMEM((2, layers, 2, 2 * lanes, 2 * lanes), jnp.bfloat16),
            pltpu.VMEM((8, 128), jnp.int32),
            pltpu.VMEM((sides, 8, 128), jnp.int32),
            pltpu.VMEM((sides + 1, 8, 128), jnp.int32),
            pltpu.SMEM((sides + 1, 8, 128), jnp.int32),
            pltpu.VMEM((2, 2 * kept, BS, BS, lanes), jnp.float32),
            pltpu.VMEM((2, steps, sides, cap // 2 * BS * BS, lanes), jnp.bfloat16),
            pltpu.VMEM((2, steps, sides, cap // 2 * BS * BS, lanes), jnp.bfloat16),
            pltpu.VMEM((2, rows, width, lanes), jnp.float32),
            pltpu.VMEM((2, own + 2 * halo, lanes), jnp.bfloat16),
            pltpu.VMEM((2, 2, 2, own + 2 * halo, lanes), jnp.bfloat16),
            pltpu.VMEM((2, frame_count, 2, halo, lanes), jnp.bfloat16),
            pltpu.VMEM((2, frame_count, 2, halo, lanes), jnp.bfloat16),
            pltpu.SemaphoreType.DMA((sides,)),
            pltpu.SemaphoreType.DMA((sides,)),
            pltpu.SemaphoreType.DMA((2, steps, sides)),
            pltpu.SemaphoreType.DMA((2, steps, sides)),
            pltpu.SemaphoreType.DMA((2, frame_count, 2)),
            pltpu.SemaphoreType.DMA((2, frame_count, 2)),
            pltpu.SemaphoreType.DMA,
        ],
        compiler_params=pltpu.CompilerParams(
            collective_id=0, has_side_effects=True, vmem_limit_bytes=56 * 1024 * 1024
        ),
    )(frames, motion_forward, motion_backward, join_weight, conv_weight)


def solution(mesh):
    return jax.shard_map(
        on_device,
        mesh=mesh,
        in_specs=(
            P(None, None, ("clips", "tiles"), None),
            P(None, ("clips", "tiles")),
            P(None, ("clips", "tiles")),
            P(),
            P(),
        ),
        out_specs=(
            P(None, None, ("clips", "tiles"), None),
            P(None, None, ("clips", "tiles"), None),
        ),
        check_vma=False,
    )
```

profile of v0, /device:TPU:11, one launch (start us, length us, event | category | flops | bytes accessed | tf_op | source)
XLA Modules:
  0.0 51.3 jit_solution(16125313560533686750)
XLA Ops:
  0.6 47.9 %shard_map.68 = (bf16[4,64,8,128]{3,2,1,0:T(8,128)(2,1)}, bf16[4,64,8,128]{3,2,1,0:T(8,128)(2,1)}) custom-call(bf16[4,64,8,128]{3,2,1,0:T(8,128)(2,1)} %frames_ref.1, s32[3,16]{1,0:T(4,128)} %mf_ref.1, s32[3,16]{1,0:T(4,128)} %mb_ref.1, bf16[2,64,128]{2,1,0:T(8,128)(2,1)} %join_ref.1, bf16[2,4,9,64,64]{4,3,2,1,0:T(8,128)(2,1)} %conv_ref.1), custom_call_target="tpu_custom_call" | custom-call | tf_op jit(solution)/shard_map/pallas_call | solution.py:446
  48.5 0.0 copy-start
  48.5 1.9 %copy.9 = bf16[4,64,8,128]{3,2,1,0:T(8,128)(2,1)} copy(bf16[4,64,8,128]{3,2,1,0:T(8,128)(2,1)} %get-tuple-element.4) | data formatting | bytes 1048576
  50.5 0.0 copy-done
  50.5 0.8 %copy.10 = bf16[4,64,8,128]{3,2,1,0:T(8,128)(2,1)} copy(bf16[4,64,8,128]{3,2,1,0:T(8,128)(2,1)S(1)} %copy-done) | data formatting | bytes 1048576
Async XLA Ops:
  48.5 1.9 %copy-start = (bf16[4,64,8,128]{3,2,1,0:T(8,128)(2,1)S(1)}, bf16[4,64,8,128]{3,2,1,0:T(8,128)(2,1)}, u32[]{:S(2)}) copy-start(bf16[4,64,8,128]{3,2,1,0:T(8,128)(2,1)} %get-tuple-element.5) | copy-start | bytes 1572868
where the time goes:
time: 51.4 us; the launch traced here: 51.3 us
  Pallas kernels  47.9 us (93%)
  local copies, waits for them, and re-layouts  2.72 us (5%)
  between operations  0.65 us (1%)
    pallas_call x1, Pallas kernels, on_device(): pl.pallas_call(functools.partial(sweep_kernel, dims), out_shape=(result,...  47.9 us
    unnamed x4, local copies, waits for them, and re-layouts  2.72 us

commit v1 on v0

v1 whole, which is shorter than its diff:
```python
import functools

import jax
import jax.numpy as jnp
from jax import lax
from jax.experimental import pallas as pl
from jax.experimental.pallas import tpu as pltpu
from jax.sharding import PartitionSpec as P

BS = 8
REACH = 2
OFFSETS = tuple(o for o in range(-REACH, REACH + 1) if o != 0)


def leaky(value):
    return jnp.maximum(value, 0.1 * value)


def blockdiag(tile):
    blank = jnp.zeros(tile.shape, tile.dtype)
    return jnp.concatenate(
        [jnp.concatenate([tile, blank], axis=1), jnp.concatenate([blank, tile], axis=1)], axis=0
    )


def matmul_t(left, right):
    return lax.dot_general(
        left, right, (((1,), (1,)), ((), ())), preferred_element_type=jnp.float32
    )


def sweep_kernel(
    dims,
    frames_hbm,
    mf_hbm,
    mb_hbm,
    join_hbm,
    conv_ref,
    ahead_ref,
    behind_ref,
    frames_ref,
    mf_ref,
    mb_ref,
    join_ref,
    conv_v,
    x_ref,
    flip,
    nat,
    wj_ref,
    wc_ref,
    mine,
    theirs,
    table_v,
    table_s,
    cand,
    packed,
    landed,
    h_ref,
    z_ref,
    edge_out,
    edge_in,
    m_send,
    m_recv,
    f_send,
    f_recv,
    e_send,
    e_recv,
    t_sem,
    w_sem,
    x_sem,
    i_sem,
):
    frame_count, rows, cols, channels, layers, devices = dims
    outs = (ahead_ref, behind_ref)
    lanes = 2 * channels
    half = cols // 2
    bc = cols // BS
    quad = BS // 2
    own_pairs = rows // 2
    margin = layers // 2
    all_pairs = own_pairs + 2 * margin
    cap = bc // (2 * REACH)
    sides = len(OFFSETS)
    lead = BS
    me = lax.axis_index("tiles")

    def present(offset):
        return (me + offset >= 0) & (me + offset < devices)

    def remote(source, target, send, receive, offset):
        return pltpu.make_async_remote_copy(
            src_ref=source,
            dst_ref=target,
            send_sem=send,
            recv_sem=receive,
            device_id={"tiles": me + offset},
            device_id_type=pl.DeviceIdType.MESH,
        )

    def motion_copy(oi, slot):
        return remote(mine, theirs.at[slot], m_send.at[oi], m_recv.at[slot], OFFSETS[oi])

    def feature_copy(d, step, oi, slot, offset):
        return remote(
            packed.at[d, step, oi], landed.at[d, step, slot],
            f_send.at[d, step, oi], f_recv.at[d, step, slot], offset,
        )

    def edge_copy(d, step, side, slot):
        return remote(
            edge_out.at[d, step, side], edge_in.at[d, step, slot],
            e_send.at[d, step, side], e_recv.at[d, step, slot], 1 if side else -1,
        )

    barrier = pltpu.get_barrier_semaphore()
    for offset in OFFSETS:
        @pl.when(present(offset))
        def _():
            pl.semaphore_signal(
                barrier, inc=1, device_id={"tiles": me + offset},
                device_id_type=pl.DeviceIdType.MESH,
            )

    first_frames = sorted({0, frame_count - 1})

    def frame_load(f):
        return pltpu.make_async_copy(frames_hbm.at[f], frames_ref.at[f], x_sem.at[f])

    small_loads = [
        pltpu.make_async_copy(source, target, i_sem.at[k])
        for k, (source, target) in enumerate(
            [(join_hbm, join_ref), (mf_hbm, mf_ref), (mb_hbm, mb_ref)]
        )
    ]
    weight_load = pltpu.make_async_copy(conv_ref, conv_v, w_sem)
    for f in first_frames:
        frame_load(f).start()
    for load in small_loads:
        load.start()
    weight_load.start()
    for f in range(1, frame_count - 1):
        frame_load(f).start()
    for oi, offset in enumerate(OFFSETS):
        @pl.when(jnp.logical_not(present(offset)))
        def _():
            theirs[oi] = jnp.full(mine.shape, -1, jnp.int32)

    for load in small_loads:
        load.wait()
    mine[...] = jnp.zeros(mine.shape, jnp.int32)
    for step in range(frame_count - 1):
        mine[step:step + 1, 0:bc] = mf_ref[step:step + 1, :]
        back = frame_count - 2 - step
        mine[frame_count - 1 + step:frame_count + step, 0:bc] = mb_ref[back:back + 1, :]

    for d in range(2):
        joined = join_ref[d]
        wj_ref[d, :, :lanes] = blockdiag(joined[:, :channels])
        wj_ref[d, :, lanes:] = blockdiag(joined[:, channels:])

    def load_frame(f):
        frame_load(f).wait()
        flip[0] = frames_ref[f].astype(jnp.float32).reshape(channels * rows, cols)
        parts = jnp.concatenate(
            [flip[0, pl.ds(r, channels, stride=rows), :] for r in range(rows)], axis=0
        ).astype(jnp.bfloat16)
        place = lax.broadcasted_iota(jnp.int32, (cols, cols), 0)
        column = lax.broadcasted_iota(jnp.int32, (cols, cols), 1)
        wanted = jnp.where(place < half, 2 * place, 2 * (place - half) + 1)
        moved = matmul_t((column == wanted).astype(jnp.bfloat16), parts).astype(jnp.bfloat16)
        for parity in range(2):
            for pair in range(own_pairs):
                x_ref[f, parity, pair * half:(pair + 1) * half, :] = moved[
                    parity * half:(parity + 1) * half, pair * lanes:(pair + 1) * lanes
                ]

    def build_weights(d):
        identity = (
            lax.broadcasted_iota(jnp.int32, (channels, channels), 0)
            == lax.broadcasted_iota(jnp.int32, (channels, channels), 1)
        ).astype(jnp.bfloat16)

        def build_layer(layer, carry):
            blank = jnp.zeros((channels, channels), jnp.bfloat16)
            for across in range(3):
                taps = [conv_v[d, layer, 3 * down + across] for down in range(3)]
                wide = jnp.concatenate(
                    [taps[0], blank, taps[1], taps[0], taps[2], taps[1], blank, taps[2]], axis=0
                )
                turned = matmul_t(identity, wide).astype(jnp.bfloat16)
                for k in range(4):
                    wc_ref[d, layer, across, k * channels:(k + 1) * channels, :] = turned[
                        :, k * lanes:(k + 1) * lanes
                    ]
            return carry

        lax.fori_loop(0, layers, build_layer, 0)

    def emit(t):
        identity = (
            lax.broadcasted_iota(jnp.int32, (lanes, lanes), 0)
            == lax.broadcasted_iota(jnp.int32, (lanes, lanes), 1)
        ).astype(jnp.bfloat16)
        for d in range(2):
            for pair in range(own_pairs):
                for parity in range(2):
                    nat[d, pl.ds(pair * cols + parity, half, stride=2), :] = cand[
                        d, 2 * pair + parity, lead:lead + half, :
                    ]
        moved = [matmul_t(identity, nat[d].astype(jnp.bfloat16)) for d in range(2)]
        for d in range(2):
            for pair in range(own_pairs):
                for low in range(2):
                    flip[d, pl.ds(2 * pair + low, channels, stride=rows), :] = moved[d][
                        low * channels:(low + 1) * channels, pair * cols:(pair + 1) * cols
                    ]
        for d in range(2):
            now = t if d == 0 else frame_count - 1 - t
            outs[d][now] = flip[d].reshape(channels, rows, cols).astype(jnp.bfloat16)

    def build_tables():
        for oi, offset in enumerate(OFFSETS):
            @pl.when(present(offset))
            def _():
                motion_copy(oi, oi).wait_send()
                motion_copy(oi, oi).wait_recv()

        depth = mine.shape[0]
        motion = mine[...]
        local = jnp.concatenate(
            [motion - (me + offset) * bc for offset in OFFSETS]
            + [theirs[oi] - me * bc for oi in range(sides)],
            axis=0,
        )
        lane = lax.broadcasted_iota(jnp.int32, local.shape, 1)
        match = (local >= 0) & (local < bc) & (lane < bc)
        flags = match.astype(jnp.int32)
        total = flags
        shift = 1
        while shift < bc:
            total = total + jnp.where(lane >= shift, pltpu.roll(total, shift, axis=1), 0)
            shift *= 2
        rank = total - flags

        mid = sides * depth
        own = motion - me * bc
        picks = jnp.where((own >= 0) & (own < bc), own, 0)
        for oi in range(sides):
            rows_of = slice(oi * depth, (oi + 1) * depth)
            code = bc + oi * cap + jnp.minimum(rank[rows_of], cap - 1)
            picks = picks + jnp.where(match[rows_of], code, 0)
        table_v[sides] = picks * quad

        wanted, order, chosen = local[mid:], rank[mid:], match[mid:]
        values = jnp.concatenate(
            [jnp.where(chosen & (order == slot), wanted, 0) for slot in range(cap)], axis=0
        )
        shift = 1
        while shift < bc + cap:
            values = values + pltpu.roll(values, shift, axis=1)
            shift *= 2
        place = lax.broadcasted_iota(jnp.int32, (mid, mine.shape[1]), 1)
        gathered = jnp.zeros(place.shape, jnp.int32)
        for slot in range(cap):
            gathered = jnp.where(place == bc + slot, values[slot * mid:(slot + 1) * mid], gathered)
        gathered = gathered * quad
        for oi in range(sides):
            table_v[oi] = gathered[oi * depth:(oi + 1) * depth]
        load = pltpu.make_async_copy(table_v, table_s, t_sem)
        load.start()
        load.wait()

    upper = lax.broadcasted_iota(jnp.int32, (BS, lanes), 0) < quad

    def two_blocks(d, k, first, second):
        return jnp.where(
            upper,
            cand[d, k, pl.ds(first + lead, BS), :],
            cand[d, k, pl.ds(second + lead - quad, BS), :],
        )

    def activate(d, slot, start, count, even, odd):
        first = start * half
        size = count * half
        z_ref[d, slot, 1, first:first + size, :] = even.astype(jnp.bfloat16)
        z_ref[d, slot, 2, first:first + size, :] = odd.astype(jnp.bfloat16)
        place = lax.broadcasted_iota(jnp.int32, (count, BS, lanes), 1)
        before = pltpu.roll(odd.reshape(count, half, lanes), 1, axis=1)
        before = jnp.concatenate(
            [jnp.where(place == 0, 0.0, before[:, :BS]), before[:, BS:]], axis=1
        )
        z_ref[d, slot, 0, first:first + size, :] = before.reshape(size, lanes).astype(jnp.bfloat16)
        after = pltpu.roll(even.reshape(count, half, lanes), half - 1, axis=1)
        after = jnp.concatenate(
            [after[:, :half - BS], jnp.where(place == BS - 1, 0.0, after[:, half - BS:])], axis=1
        )
        z_ref[d, slot, 3, first:first + size, :] = after.reshape(size, lanes).astype(jnp.bfloat16)

    def send_edges(d, t, first):
        size = own_pairs * half
        edge = margin * half
        for parity in range(2):
            base = parity * size
            edge_out[d, t, 0, parity] = first[base:base + edge]
            edge_out[d, t, 1, parity] = first[base + size - edge:base + size]
        for side in range(2):
            @pl.when(present(1 if side else -1))
            def _():
                edge_copy(d, t, side, 1 - side).start()
        wide = first.astype(jnp.float32)
        h_ref[d, 0, 0, edge:edge + size, :] = wide[:size]
        h_ref[d, 0, 1, edge:edge + size, :] = wide[size:]
        wide = leaky(wide)
        activate(d, 0, margin, own_pairs, wide[:size], wide[size:])

    def begin_first(d):
        now = 0 if d == 0 else frame_count - 1
        both = jnp.concatenate([x_ref[now, 0], x_ref[now, 1]], axis=0)
        send_edges(d, 0, matmul_t(both, wj_ref[d, :, lanes:]).astype(jnp.bfloat16))

    def begin(d, t):
        step = t - 1
        row = d * (frame_count - 1) + step
        for oi, offset in enumerate(OFFSETS):
            @pl.when(present(offset))
            def _():
                feature_copy(d, step, oi, oi, offset).wait_recv()
                at = lead + (bc + oi * cap) * quad
                for k in range(2 * own_pairs):
                    cand[d, k, at:at + cap * quad, :] = landed[d, step, oi, k].astype(jnp.float32)
        picks = [table_s[sides, row, j] for j in range(bc)]
        now = t if d == 0 else frame_count - 1 - t
        parts = []
        for parity in range(2):
            tiles = [
                two_blocks(d, 2 * pair + parity, picks[2 * j], picks[2 * j + 1])
                for pair in range(own_pairs)
                for j in range(bc // 2)
            ]
            taken = jnp.concatenate(tiles, axis=0).astype(jnp.bfloat16)
            parts.append(jnp.concatenate([taken, x_ref[now, parity]], axis=1))
        both = jnp.concatenate(parts, axis=0)
        send_edges(d, t, matmul_t(both, wj_ref[d]).astype(jnp.bfloat16))

    top_inside = (me > 0).astype(jnp.float32)
    bottom_inside = (me < devices - 1).astype(jnp.float32)

    low_lanes = lax.broadcasted_iota(jnp.int32, (1, lanes), 1) < channels
    top_mixed = jnp.where(low_lanes, top_inside, 1.0)
    bottom_mixed = jnp.where(low_lanes, 1.0, bottom_inside)

    def inside(value, layer, begin_pair):
        count = value.shape[0] // half
        pieces = []
        for q in range(count):
            start = 2 * (q + begin_pair) + layer + 1 - layers
            piece = value[q * half:(q + 1) * half]
            if start + 1 < 0:
                piece = piece * top_inside
            elif start < 0:
                piece = piece * top_mixed
            elif start >= rows:
                piece = piece * bottom_inside
            elif start + 1 >= rows:
                piece = piece * bottom_mixed
            pieces.append(piece)
        return jnp.concatenate(pieces, axis=0)

    def multiply(d, layer, first, last):
        now = layer % 2
        base = first * half
        size = (last - first) * half
        left = jnp.concatenate(
            [
                z_ref[d, now, k, base + low * half:base + low * half + size, :]
                for k in range(4)
                for low in range(2)
            ],
            axis=1,
        )
        taps = [wc_ref[d, layer, across] for across in range(3)]
        blank = jnp.zeros(taps[0].shape, jnp.bfloat16)
        right = jnp.concatenate(
            [
                jnp.concatenate([taps[0], blank], axis=1),
                jnp.concatenate([taps[1], taps[0]], axis=1),
                jnp.concatenate([taps[2], taps[1]], axis=1),
                jnp.concatenate([blank, taps[2]], axis=1),
            ],
            axis=0,
        )
        return jnp.dot(left, right, preferred_element_type=jnp.float32)

    def settle(d, layer, first, last, summed):
        now, later = layer % 2, (layer + 1) % 2
        count = last - first
        base = first * half
        size = count * half
        first_half = lax.broadcasted_iota(jnp.int32, (size, lanes), 1) < channels
        fresh = []
        for parity in range(2):
            kept = jnp.where(
                first_half,
                h_ref[d, now, parity, base + half:base + half + size, :],
                h_ref[d, now, parity, base:base + size, :],
            )
            fresh.append(
                pltpu.roll(kept, channels, axis=1) + summed[:, parity * lanes:(parity + 1) * lanes]
            )
        if layer < layers - 1:
            for parity in range(2):
                h_ref[d, later, parity, base:base + size, :] = fresh[parity]
            activate(
                d, later, first, count,
                inside(leaky(fresh[0]), layer, first), inside(leaky(fresh[1]), layer, first),
            )
        else:
            for parity in range(2):
                rounded = fresh[parity].astype(jnp.bfloat16).astype(jnp.float32)
                for pair in range(first, last):
                    at = (pair - first) * half
                    cand[d, 2 * pair + parity, lead:lead + half, :] = rounded[at:at + half]

    def finish(d, t):
        edge = margin * half
        for side in range(2):
            pair = side * (margin + own_pairs)
            start = pair * half

            @pl.when(present(1 if side else -1))
            def _():
                edge_copy(d, t, side, side).wait_recv()
                even = edge_in[d, t, side, 0].astype(jnp.float32)
                odd = edge_in[d, t, side, 1].astype(jnp.float32)
                h_ref[d, 0, 0, start:start + edge, :] = even
                h_ref[d, 0, 1, start:start + edge, :] = odd
                activate(d, 0, pair, margin, leaky(even), leaky(odd))

            @pl.when(jnp.logical_not(present(1 if side else -1)))
            def _():
                for parity in range(2):
                    h_ref[d, 0, parity, start:start + edge, :] = jnp.zeros((edge, lanes), jnp.float32)
                for k in range(4):
                    z_ref[d, 0, k, start:start + edge, :] = jnp.zeros((edge, lanes), jnp.bfloat16)

        for layer in range(layers):
            settle(d, layer, 0, all_pairs - 1 - layer, multiply(d, layer, 0, all_pairs - 1 - layer))

        @pl.when(t < frame_count - 1)
        def _():
            row = d * (frame_count - 1) + t
            for oi, offset in enumerate(OFFSETS):
                picks = [table_s[oi, row, bc + slot] for slot in range(cap)]
                for k in range(2 * own_pairs):
                    packed[d, t, oi, k] = jnp.concatenate(
                        [
                            two_blocks(d, k, picks[slot], picks[slot + 1])
                            for slot in range(0, cap, 2)
                        ],
                        axis=0,
                    ).astype(jnp.bfloat16)
            flag = (me // 2) % 2
            for k in range(sides):
                oi = k + flag * (sides - 1 - 2 * k)
                offset = oi - REACH + (oi + REACH) // (2 * REACH)

                @pl.when(present(offset))
                def _():
                    feature_copy(d, t, oi, sides - 1 - oi, offset).start()

    for f in first_frames:
        load_frame(f)

    peers = jnp.minimum(me, REACH) + jnp.minimum(devices - 1 - me, REACH)
    pl.semaphore_wait(barrier, peers)

    for oi, offset in enumerate(OFFSETS):
        @pl.when(present(offset))
        def _():
            motion_copy(oi, sides - 1 - oi).start()
    for d in range(2):
        begin_first(d)

    def load_rest(f, carry):
        load_frame(f)
        return carry

    lax.fori_loop(1, frame_count - 1, load_rest, 0)
    weight_load.wait()
    for d in range(2):
        build_weights(d)
    build_tables()

    def frame_step(t, carry):
        finish(0, t)
        finish(1, t)
        emit(t)

        @pl.when(t < frame_count - 1)
        def _():
            begin(0, t + 1)
            begin(1, t + 1)

        return carry

    lax.fori_loop(0, frame_count, frame_step, 0)

    for d in range(2):
        for step in range(frame_count):
            for side in range(2):
                @pl.when(present(1 if side else -1))
                def _():
                    edge_copy(d, step, side, side).wait_send()
            if step < frame_count - 1:
                for oi, offset in enumerate(OFFSETS):
                    @pl.when(present(offset))
                    def _():
                        feature_copy(d, step, oi, oi, offset).wait_send()


def on_device(frames, motion_forward, motion_backward, join_weight, conv_weight):
    frame_count, channels, rows, cols = frames.shape
    layers = conv_weight.shape[1]
    devices = lax.axis_size("tiles")
    lanes = 2 * channels
    half = cols // 2
    bc = rows // BS * (cols // BS)
    cap = bc // (2 * REACH)
    sides = len(OFFSETS)
    steps = frame_count - 1
    own_pairs = rows // 2
    margin = layers // 2
    all_pairs = own_pairs + 2 * margin
    quad = BS // 2
    reach = 2 * BS + (bc + sides * cap) * quad

    dims = (frame_count, rows, cols, channels, layers, devices)
    vmem = pl.BlockSpec(memory_space=pltpu.VMEM)
    result = pltpu.VMEM(frames.shape, jnp.bfloat16)
    block = (2 * own_pairs, cap * quad, lanes)
    edge = (2, margin * half, lanes)
    return pl.pallas_call(
        functools.partial(sweep_kernel, dims),
        out_shape=(result, result),
        in_specs=[pl.BlockSpec(memory_space=pltpu.HBM)] * 5,
        out_specs=(vmem, vmem),
        scratch_shapes=[
            pltpu.VMEM(frames.shape, jnp.bfloat16),
            pltpu.VMEM(motion_forward.shape, jnp.int32),
            pltpu.VMEM(motion_backward.shape, jnp.int32),
            pltpu.VMEM(join_weight.shape, jnp.bfloat16),
            pltpu.VMEM(conv_weight.shape, jnp.bfloat16),
            pltpu.VMEM((frame_count, 2, own_pairs * half, lanes), jnp.bfloat16),
            pltpu.VMEM((2, channels * rows, cols), jnp.float32),
            pltpu.VMEM((2, own_pairs * cols, lanes), jnp.float32),
            pltpu.VMEM((2, lanes, 2 * lanes), jnp.bfloat16),
            pltpu.VMEM((2, layers, 3, 2 * lanes, lanes), jnp.bfloat16),
            pltpu.VMEM((8, 128), jnp.int32),
            pltpu.VMEM((sides, 8, 128), jnp.int32),
            pltpu.VMEM((sides + 1, 8, 128), jnp.int32),
            pltpu.SMEM((sides + 1, 8, 128), jnp.int32),
            pltpu.VMEM((2, 2 * own_pairs, reach, lanes), jnp.float32),
            pltpu.VMEM((2, steps, sides, *block), jnp.bfloat16),
            pltpu.VMEM((2, steps, sides, *block), jnp.bfloat16),
            pltpu.VMEM((2, 2, 2, all_pairs * half, lanes), jnp.float32),
            pltpu.VMEM((2, 2, 4, all_pairs * half, lanes), jnp.bfloat16),
            pltpu.VMEM((2, frame_count, 2, *edge), jnp.bfloat16),
            pltpu.VMEM((2, frame_count, 2, *edge), jnp.bfloat16),
            pltpu.SemaphoreType.DMA((sides,)),
            pltpu.SemaphoreType.DMA((sides,)),
            pltpu.SemaphoreType.DMA((2, steps, sides)),
            pltpu.SemaphoreType.DMA((2, steps, sides)),
            pltpu.SemaphoreType.DMA((2, frame_count, 2)),
            pltpu.SemaphoreType.DMA((2, frame_count, 2)),
            pltpu.SemaphoreType.DMA,
            pltpu.SemaphoreType.DMA,
            pltpu.SemaphoreType.DMA((frame_count,)),
            pltpu.SemaphoreType.DMA((3,)),
        ],
        compiler_params=pltpu.CompilerParams(
            collective_id=0, has_side_effects=True, vmem_limit_bytes=60 * 1024 * 1024
        ),
    )(frames, motion_forward, motion_backward, join_weight, conv_weight)


def solution(mesh):
    return jax.shard_map(
        on_device,
        mesh=mesh,
        in_specs=(
            P(None, None, ("clips", "tiles"), None),
            P(None, ("clips", "tiles")),
            P(None, ("clips", "tiles")),
            P(),
            P(),
        ),
        out_specs=(
            P(None, None, ("clips", "tiles"), None),
            P(None, None, ("clips", "tiles"), None),
        ),
        check_vma=False,
    )
```

time: 51.4 us -> 44.8 us (0.87)
  Pallas kernels: 47.9 us -> 42.4 us
  local copies, waits for them, and re-layouts: 2.72 us -> 1.59 us
    pallas_call x1, Pallas kernels: 47.9 us -> 42.4 us  [on_device(): pl.pallas_call(functools.partial(sweep_kernel, dims), out_shape=(result,...]
    unnamed x4 -> x2, local copies, waits for them, and re-layouts: 2.72 us -> 1.59 us
where the time goes in v1:
time: 44.8 us; the launch traced here: 44.6 us
  Pallas kernels  42.4 us (95%)
  local copies, waits for them, and re-layouts  1.59 us (4%)
  between operations  0.64 us (1%)
    pallas_call x1, Pallas kernels, on_device(): pl.pallas_call(functools.partial(sweep_kernel, dims), out_shape=(result,...  42.4 us
    unnamed x2, local copies, waits for them, and re-layouts  1.59 us

profile of v1, /device:TPU:11, one launch (start us, length us, event | category | flops | bytes accessed | tf_op | source)
XLA Modules:
  0.0 44.6 jit_solution(17774060476056997695)
XLA Ops:
  0.6 42.4 %shard_map.68 = (bf16[4,64,8,128]{3,2,1,0:T(8,128)(2,1)S(1)}, bf16[4,64,8,128]{3,2,1,0:T(8,128)(2,1)S(1)}) custom-call(bf16[4,64,8,128]{3,2,1,0:T(8,128)(2,1)} %frames_hbm.1, s32[3,16]{1,0:T(4,128)} %mf_hbm.1, s32[3,16]{1,0:T(4,128)} %mb_hbm.1, bf16[2,64,128]{2,1,0:T(8,128)(2,1)} %join_hbm.1, bf16[2,4,9,64,64]{4,3,2,1,0:T(8,128)(2,1)} %conv_ref.1), custom_call_target="tpu_custom_call" | custom-call | tf_op jit(solution)/shard_map/pallas_call | solution.py:542
  43.0 0.8 %copy.9 = bf16[4,64,8,128]{3,2,1,0:T(8,128)(2,1)} copy(bf16[4,64,8,128]{3,2,1,0:T(8,128)(2,1)S(1)} %get-tuple-element.2) | data formatting | bytes 1048576
  43.8 0.8 %copy.10 = bf16[4,64,8,128]{3,2,1,0:T(8,128)(2,1)} copy(bf16[4,64,8,128]{3,2,1,0:T(8,128)(2,1)S(1)} %get-tuple-element.3) | data formatting | bytes 1048576

commit v2 on v1

--- a/solution.py
+++ b/solution.py
@@ -60,15 +60,11 @@
     edge_out,
     edge_in,
     m_send,
-    m_recv,
     f_send,
     f_recv,
     e_send,
     e_recv,
-    t_sem,
-    w_sem,
     x_sem,
-    i_sem,
 ):
     frame_count, rows, cols, channels, layers, devices = dims
     outs = (ahead_ref, behind_ref)
@@ -98,18 +94,18 @@
         )
 
     def motion_copy(oi, slot):
-        return remote(mine, theirs.at[slot], m_send.at[oi], m_recv.at[slot], OFFSETS[oi])
+        return remote(mine, theirs.at[slot], m_send.at[oi], f_recv.at[1, 1, slot], OFFSETS[oi])
 
     def feature_copy(d, step, oi, slot, offset):
         return remote(
             packed.at[d, step, oi], landed.at[d, step, slot],
-            f_send.at[d, step, oi], f_recv.at[d, step, slot], offset,
+            f_send.at[d, oi], f_recv.at[d, step % 2, slot], offset,
         )
 
     def edge_copy(d, step, side, slot):
         return remote(
             edge_out.at[d, step, side], edge_in.at[d, step, slot],
-            e_send.at[d, step, side], e_recv.at[d, step, slot], 1 if side else -1,
+            e_send.at[d, side], e_recv.at[d, slot], 1 if side else -1,
         )
 
     barrier = pltpu.get_barrier_semaphore()
@@ -127,12 +123,12 @@
         return pltpu.make_async_copy(frames_hbm.at[f], frames_ref.at[f], x_sem.at[f])
 
     small_loads = [
-        pltpu.make_async_copy(source, target, i_sem.at[k])
+        pltpu.make_async_copy(source, target, f_send.at[1, k])
         for k, (source, target) in enumerate(
             [(join_hbm, join_ref), (mf_hbm, mf_ref), (mb_hbm, mb_ref)]
         )
     ]
-    weight_load = pltpu.make_async_copy(conv_ref, conv_v, w_sem)
+    weight_load = pltpu.make_async_copy(conv_ref, conv_v, f_send.at[0, 0])
     for f in first_frames:
         frame_load(f).start()
     for load in small_loads:
@@ -266,7 +262,7 @@
         gathered = gathered * quad
         for oi in range(sides):
             table_v[oi] = gathered[oi * depth:(oi + 1) * depth]
-        load = pltpu.make_async_copy(table_v, table_s, t_sem)
+        load = pltpu.make_async_copy(table_v, table_s, f_send.at[0, 1])
         load.start()
         load.wait()
 
@@ -341,6 +337,10 @@
             parts.append(jnp.concatenate([taken, x_ref[now, parity]], axis=1))
         both = jnp.concatenate(parts, axis=0)
         send_edges(d, t, matmul_t(both, wj_ref[d]).astype(jnp.bfloat16))
+        for oi, offset in enumerate(OFFSETS):
+            @pl.when(present(offset))
+            def _():
+                feature_copy(d, step, oi, oi, offset).wait_send()
 
     top_inside = (me > 0).astype(jnp.float32)
     bottom_inside = (me < devices - 1).astype(jnp.float32)
@@ -443,8 +443,15 @@
                 for k in range(4):
                     z_ref[d, 0, k, start:start + edge, :] = jnp.zeros((edge, lanes), jnp.bfloat16)
 
+        spans = []
         for layer in range(layers):
-            settle(d, layer, 0, all_pairs - 1 - layer, multiply(d, layer, 0, all_pairs - 1 - layer))
+            split = layers - layer
+            spans += [(layer, 0, split), (layer, split, all_pairs - 1 - layer)]
+        pending = [multiply(d, *spans[0])]
+        for k, span in enumerate(spans):
+            if k + 1 < len(spans):
+                pending.append(multiply(d, *spans[k + 1]))
+            settle(d, *span, pending[k])
 
         @pl.when(t < frame_count - 1)
         def _():
@@ -468,6 +475,11 @@
                 def _():
                     feature_copy(d, t, oi, sides - 1 - oi, offset).start()
 
+        for side in range(2):
+            @pl.when(present(1 if side else -1))
+            def _():
+                edge_copy(d, t, side, side).wait_send()
+
     for f in first_frames:
         load_frame(f)
 
@@ -505,17 +517,17 @@
 
     lax.fori_loop(0, frame_count, frame_step, 0)
 
-    for d in range(2):
-        for step in range(frame_count):
-            for side in range(2):
-                @pl.when(present(1 if side else -1))
-                def _():
-                    edge_copy(d, step, side, side).wait_send()
-            if step < frame_count - 1:
-                for oi, offset in enumerate(OFFSETS):
-                    @pl.when(present(offset))
-                    def _():
-                        feature_copy(d, step, oi, oi, offset).wait_send()
+
+def store_kernel(ahead_ref, behind_ref, ahead_out, behind_out, sems):
+    copies = [
+        pltpu.make_async_copy(source.at[f], target.at[f], sems.at[k, f])
+        for k, (source, target) in enumerate([(ahead_ref, ahead_out), (behind_ref, behind_out)])
+        for f in range(source.shape[0])
+    ]
+    for copy in copies:
+        copy.start()
+    for copy in copies:
+        copy.wait()
 
 
 def on_device(frames, motion_forward, motion_backward, join_weight, conv_weight):
@@ -539,7 +551,7 @@
     result = pltpu.VMEM(frames.shape, jnp.bfloat16)
     block = (2 * own_pairs, cap * quad, lanes)
     edge = (2, margin * half, lanes)
-    return pl.pallas_call(
+    swept = pl.pallas_call(
         functools.partial(sweep_kernel, dims),
         out_shape=(result, result),
         in_specs=[pl.BlockSpec(memory_space=pltpu.HBM)] * 5,
@@ -567,20 +579,26 @@
             pltpu.VMEM((2, frame_count, 2, *edge), jnp.bfloat16),
             pltpu.VMEM((2, frame_count, 2, *edge), jnp.bfloat16),
             pltpu.SemaphoreType.DMA((sides,)),
-            pltpu.SemaphoreType.DMA((sides,)),
-            pltpu.SemaphoreType.DMA((2, steps, sides)),
-            pltpu.SemaphoreType.DMA((2, steps, sides)),
-            pltpu.SemaphoreType.DMA((2, frame_count, 2)),
-            pltpu.SemaphoreType.DMA((2, frame_count, 2)),
-            pltpu.SemaphoreType.DMA,
-            pltpu.SemaphoreType.DMA,
+            pltpu.SemaphoreType.DMA((2, sides)),
+            pltpu.SemaphoreType.DMA((2, 2, sides)),
+            pltpu.SemaphoreType.DMA((2, 2)),
+            pltpu.SemaphoreType.DMA((2, 2)),
             pltpu.SemaphoreType.DMA((frame_count,)),
-            pltpu.SemaphoreType.DMA((3,)),
         ],
         compiler_params=pltpu.CompilerParams(
             collective_id=0, has_side_effects=True, vmem_limit_bytes=60 * 1024 * 1024
         ),
     )(frames, motion_forward, motion_backward, join_weight, conv_weight)
+    outside = pl.BlockSpec(memory_space=pltpu.HBM)
+    plain = jax.ShapeDtypeStruct(frames.shape, jnp.bfloat16)
+    return pl.pallas_call(
+        store_kernel,
+        out_shape=(plain, plain),
+        in_specs=[pl.BlockSpec(memory_space=pl.ANY)] * 2,
+        out_specs=(outside, outside),
+        scratch_shapes=[pltpu.SemaphoreType.DMA((2, frame_count))],
+        compiler_params=pltpu.CompilerParams(vmem_limit_bytes=4 * 1024 * 1024),
+    )(*swept)
 
 
 def solution(mesh):

time: 44.8 us -> 41.7 us (0.931)
  Pallas kernels: 42.4 us -> 40.8 us
  local copies, waits for them, and re-layouts: 1.59 us -> 0 us
    pallas_call x1, Pallas kernels: 42.4 us -> 39.8 us  [on_device(): pl.pallas_call(functools.partial(sweep_kernel, dims), out_shape=(result,...]
    unnamed x2 -> x0, local copies, waits for them, and re-layouts: 1.59 us -> none
    pallas_call x0 -> x1, Pallas kernels: none -> 1.03 us  [on_device(): pl.pallas_call(store_kernel, out_shape=(plain, plain), in_specs=[pl.Block...]
where the time goes in v2:
time: 41.7 us; the launch traced here: 41.4 us
  Pallas kernels  40.8 us (98%)
  between operations  0.64 us (2%)
    pallas_call x1, Pallas kernels, on_device(): pl.pallas_call(functools.partial(sweep_kernel, dims), out_shape=(result,...  39.8 us
    pallas_call x1, Pallas kernels, on_device(): pl.pallas_call(store_kernel, out_shape=(plain, plain), in_specs=[pl.Block...  1.03 us

profile of v2, /device:TPU:11, one launch (start us, length us, event | category | flops | bytes accessed | tf_op | source)
XLA Modules:
  0.0 41.4 jit_solution(6937137518654358564)
XLA Ops:
  0.6 39.8 %shard_map.68 = (bf16[4,64,8,128]{3,2,1,0:T(8,128)(2,1)S(1)}, bf16[4,64,8,128]{3,2,1,0:T(8,128)(2,1)S(1)}) custom-call(bf16[4,64,8,128]{3,2,1,0:T(8,128)(2,1)} %frames_hbm.1, s32[3,16]{1,0:T(4,128)} %mf_hbm.1, s32[3,16]{1,0:T(4,128)} %mb_hbm.1, bf16[2,64,128]{2,1,0:T(8,128)(2,1)} %join_hbm.1, bf16[2,4,9,64,64]{4,3,2,1,0:T(8,128)(2,1)} %conv_ref.1), custom_call_target="tpu_custom_call" | custom-call | tf_op jit(solution)/shard_map/pallas_call | solution.py:554
  40.4 1.0 %shard_map.69 = (bf16[4,64,8,128]{3,2,1,0:T(8,128)(2,1)}, bf16[4,64,8,128]{3,2,1,0:T(8,128)(2,1)}) custom-call(bf16[4,64,8,128]{3,2,1,0:T(8,128)(2,1)S(1)} %get-tuple-element.4.ahead_ref, bf16[4,64,8,128]{3,2,1,0:T(8,128)(2,1)S(1)} %get-tuple-element.5.behind_ref), custom_call_target="tpu_custom_call" | custom-call | tf_op jit(solution)/shard_map/pallas_call | solution.py:594

commit v3 on v2

--- a/solution.py
+++ b/solution.py
@@ -108,15 +108,6 @@
             e_send.at[d, side], e_recv.at[d, slot], 1 if side else -1,
         )
 
-    barrier = pltpu.get_barrier_semaphore()
-    for offset in OFFSETS:
-        @pl.when(present(offset))
-        def _():
-            pl.semaphore_signal(
-                barrier, inc=1, device_id={"tiles": me + offset},
-                device_id_type=pl.DeviceIdType.MESH,
-            )
-
     first_frames = sorted({0, frame_count - 1})
 
     def frame_load(f):
@@ -136,6 +127,15 @@
     weight_load.start()
     for f in range(1, frame_count - 1):
         frame_load(f).start()
+    barrier = pltpu.get_barrier_semaphore()
+    for offset in OFFSETS:
+        @pl.when(present(offset))
+        def _():
+            pl.semaphore_signal(
+                barrier, inc=1, device_id={"tiles": me + offset},
+                device_id_type=pl.DeviceIdType.MESH,
+            )
+
     for oi, offset in enumerate(OFFSETS):
         @pl.when(jnp.logical_not(present(offset)))
         def _():
@@ -170,24 +170,38 @@
                     parity * half:(parity + 1) * half, pair * lanes:(pair + 1) * lanes
                 ]
 
-    def build_weights(d):
+    def build_weights():
         identity = (
             lax.broadcasted_iota(jnp.int32, (channels, channels), 0)
             == lax.broadcasted_iota(jnp.int32, (channels, channels), 1)
         ).astype(jnp.bfloat16)
+        low = lax.broadcasted_iota(jnp.int32, (channels, lanes), 1) < channels
 
         def build_layer(layer, carry):
-            blank = jnp.zeros((channels, channels), jnp.bfloat16)
-            for across in range(3):
-                taps = [conv_v[d, layer, 3 * down + across] for down in range(3)]
+            for d in range(2):
                 wide = jnp.concatenate(
-                    [taps[0], blank, taps[1], taps[0], taps[2], taps[1], blank, taps[2]], axis=0
+                    [
+                        conv_v[d, layer, 3 * down + across]
+                        for across in range(3)
+                        for down in (1, 0, 2, 1)
+                    ],
+                    axis=0,
                 )
-                turned = matmul_t(identity, wide).astype(jnp.bfloat16)
-                for k in range(4):
-                    wc_ref[d, layer, across, k * channels:(k + 1) * channels, :] = turned[
-                        :, k * lanes:(k + 1) * lanes
+                turned = matmul_t(identity, wide)
+                for across in range(3):
+                    at = 2 * across * lanes
+                    upper_pair = turned[:, at:at + lanes]
+                    lower_pair = turned[:, at + lanes:at + 2 * lanes]
+                    blocks = [
+                        jnp.where(low, pltpu.roll(upper_pair, channels, axis=1), 0.0),
+                        upper_pair,
+                        lower_pair,
+                        jnp.where(low, 0.0, pltpu.roll(lower_pair, channels, axis=1)),
                     ]
+                    for k, block in enumerate(blocks):
+                        wc_ref[d, layer, across, k * channels:(k + 1) * channels, :] = block.astype(
+                            jnp.bfloat16
+                        )
             return carry
 
         lax.fori_loop(0, layers, build_layer, 0)
@@ -214,6 +228,8 @@
             now = t if d == 0 else frame_count - 1 - t
             outs[d][now] = flip[d].reshape(channels, rows, cols).astype(jnp.bfloat16)
 
+    table_load = pltpu.make_async_copy(table_v, table_s, m_send.at[0])
+
     def build_tables():
         for oi, offset in enumerate(OFFSETS):
             @pl.when(present(offset))
@@ -262,9 +278,7 @@
         gathered = gathered * quad
         for oi in range(sides):
             table_v[oi] = gathered[oi * depth:(oi + 1) * depth]
-        load = pltpu.make_async_copy(table_v, table_s, f_send.at[0, 1])
-        load.start()
-        load.wait()
+        table_load.start()
 
     upper = lax.broadcasted_iota(jnp.int32, (BS, lanes), 0) < quad
 
@@ -366,17 +380,21 @@
             pieces.append(piece)
         return jnp.concatenate(pieces, axis=0)
 
-    def multiply(d, layer, first, last):
-        now = layer % 2
-        base = first * half
-        size = (last - first) * half
+    def multiply(d, layer, spans):
+        now = layer
         left = jnp.concatenate(
             [
-                z_ref[d, now, k, base + low * half:base + low * half + size, :]
-                for k in range(4)
-                for low in range(2)
+                jnp.concatenate(
+                    [
+                        z_ref[d, now, k, (first + low) * half:(last + low) * half, :]
+                        for k in range(4)
+                        for low in range(2)
+                    ],
+                    axis=1,
+                )
+                for first, last in spans
             ],
-            axis=1,
+            axis=0,
         )
         taps = [wc_ref[d, layer, across] for across in range(3)]
         blank = jnp.zeros(taps[0].shape, jnp.bfloat16)
@@ -389,10 +407,32 @@
             ],
             axis=0,
         )
-        return jnp.dot(left, right, preferred_element_type=jnp.float32)
+        summed = jnp.dot(left, right, preferred_element_type=jnp.float32)
+        parts, at = [], 0
+        for first, last in spans:
+            parts.append(summed[at:at + (last - first) * half])
+            at += (last - first) * half
+        return parts
+
+    def run(d, jobs, ahead):
+        pending = [multiply(d, *jobs[0])]
+        for k, (layer, spans) in enumerate(jobs):
+            if k + 1 < len(jobs) and ahead:
+                pending.append(multiply(d, *jobs[k + 1]))
+            for span, summed in zip(spans, pending[k]):
+                settle(d, layer, *span, summed)
+            if k + 1 < len(jobs) and not ahead:
+                pending.append(multiply(d, *jobs[k + 1]))
+
+    def inner_end(layer):
+        return all_pairs - margin - 1 - layer
+
+    def inner(d):
+        jobs = [(layer, [(margin, inner_end(layer))]) for layer in range(layers)]
+        run(d, [job for job in jobs if job[1][0][1] > margin], False)
 
     def settle(d, layer, first, last, summed):
-        now, later = layer % 2, (layer + 1) % 2
+        now, later = layer, layer + 1
         count = last - first
         base = first * half
         size = count * half
@@ -443,33 +483,34 @@
                 for k in range(4):
                     z_ref[d, 0, k, start:start + edge, :] = jnp.zeros((edge, lanes), jnp.bfloat16)
 
-        spans = []
+        jobs = []
         for layer in range(layers):
-            split = layers - layer
-            spans += [(layer, 0, split), (layer, split, all_pairs - 1 - layer)]
-        pending = [multiply(d, *spans[0])]
-        for k, span in enumerate(spans):
-            if k + 1 < len(spans):
-                pending.append(multiply(d, *spans[k + 1]))
-            settle(d, *span, pending[k])
+            top = (0, margin)
+            bottom = (max(margin, inner_end(layer)), all_pairs - 1 - layer)
+            jobs += [(layer, [top]), (layer, [bottom])]
+        run(d, jobs, True)
+
+        if d == 0:
+            @pl.when(t == 0)
+            def _():
+                table_load.wait()
 
         @pl.when(t < frame_count - 1)
         def _():
             row = d * (frame_count - 1) + t
-            for oi, offset in enumerate(OFFSETS):
+            flag = (me // 2) % 2
+            for k in range(sides):
+                oi = k + flag * (sides - 1 - 2 * k)
+                offset = oi - REACH + (oi + REACH) // (2 * REACH)
                 picks = [table_s[oi, row, bc + slot] for slot in range(cap)]
-                for k in range(2 * own_pairs):
-                    packed[d, t, oi, k] = jnp.concatenate(
+                for tile in range(2 * own_pairs):
+                    packed[d, t, oi, tile] = jnp.concatenate(
                         [
-                            two_blocks(d, k, picks[slot], picks[slot + 1])
+                            two_blocks(d, tile, picks[slot], picks[slot + 1])
                             for slot in range(0, cap, 2)
                         ],
                         axis=0,
                     ).astype(jnp.bfloat16)
-            flag = (me // 2) % 2
-            for k in range(sides):
-                oi = k + flag * (sides - 1 - 2 * k)
-                offset = oi - REACH + (oi + REACH) // (2 * REACH)
 
                 @pl.when(present(offset))
                 def _():
@@ -497,20 +538,26 @@
         load_frame(f)
         return carry
 
-    lax.fori_loop(1, frame_count - 1, load_rest, 0)
     weight_load.wait()
-    for d in range(2):
-        build_weights(d)
+    build_weights()
+    inner(0)
     build_tables()
 
     def frame_step(t, carry):
         finish(0, t)
+        inner(1)
         finish(1, t)
+
+        @pl.when(t == 0)
+        def _():
+            lax.fori_loop(1, frame_count - 1, load_rest, 0)
+
         emit(t)
 
         @pl.when(t < frame_count - 1)
         def _():
             begin(0, t + 1)
+            inner(0)
             begin(1, t + 1)
 
         return carry
@@ -574,8 +621,8 @@
             pltpu.VMEM((2, 2 * own_pairs, reach, lanes), jnp.float32),
             pltpu.VMEM((2, steps, sides, *block), jnp.bfloat16),
             pltpu.VMEM((2, steps, sides, *block), jnp.bfloat16),
-            pltpu.VMEM((2, 2, 2, all_pairs * half, lanes), jnp.float32),
-            pltpu.VMEM((2, 2, 4, all_pairs * half, lanes), jnp.bfloat16),
+            pltpu.VMEM((2, layers, 2, all_pairs * half, lanes), jnp.float32),
+            pltpu.VMEM((2, layers, 4, all_pairs * half, lanes), jnp.bfloat16),
             pltpu.VMEM((2, frame_count, 2, *edge), jnp.bfloat16),
             pltpu.VMEM((2, frame_count, 2, *edge), jnp.bfloat16),
             pltpu.SemaphoreType.DMA((sides,)),

time: 41.7 us -> 40.2 us (0.964)
  Pallas kernels: 40.8 us -> 39.4 us
    pallas_call x1, Pallas kernels: 39.8 us -> 38.4 us  [on_device(): pl.pallas_call(functools.partial(sweep_kernel, dims), out_shape=(result,...]
where the time goes in v3:
time: 40.2 us; the launch traced here: 40.1 us
  Pallas kernels  39.4 us (98%)
  between operations  0.64 us (2%)
    pallas_call x1, Pallas kernels, on_device(): pl.pallas_call(functools.partial(sweep_kernel, dims), out_shape=(result,...  38.4 us
    pallas_call x1, Pallas kernels, on_device(): pl.pallas_call(store_kernel, out_shape=(plain, plain), in_specs=[pl.Block...  1.03 us

profile of v3, /device:TPU:11, one launch (start us, length us, event | category | flops | bytes accessed | tf_op | source)
XLA Modules:
  0.0 40.1 jit_solution(6262286821583821223)
XLA Ops:
  0.6 38.4 %shard_map.68 = (bf16[4,64,8,128]{3,2,1,0:T(8,128)(2,1)S(1)}, bf16[4,64,8,128]{3,2,1,0:T(8,128)(2,1)S(1)}) custom-call(bf16[4,64,8,128]{3,2,1,0:T(8,128)(2,1)} %frames_hbm.1, s32[3,16]{1,0:T(4,128)} %mf_hbm.1, s32[3,16]{1,0:T(4,128)} %mb_hbm.1, bf16[2,64,128]{2,1,0:T(8,128)(2,1)} %join_hbm.1, bf16[2,4,9,64,64]{4,3,2,1,0:T(8,128)(2,1)} %conv_ref.1), custom_call_target="tpu_custom_call" | custom-call | tf_op jit(solution)/shard_map/pallas_call | solution.py:601
  39.1 1.0 %shard_map.69 = (bf16[4,64,8,128]{3,2,1,0:T(8,128)(2,1)}, bf16[4,64,8,128]{3,2,1,0:T(8,128)(2,1)}) custom-call(bf16[4,64,8,128]{3,2,1,0:T(8,128)(2,1)S(1)} %get-tuple-element.4.ahead_ref, bf16[4,64,8,128]{3,2,1,0:T(8,128)(2,1)S(1)} %get-tuple-element.5.behind_ref), custom_call_target="tpu_custom_call" | custom-call | tf_op jit(solution)/shard_map/pallas_call | solution.py:641

commit v4 on v3

--- a/solution.py
+++ b/solution.py
@@ -461,6 +461,15 @@
                     at = (pair - first) * half
                     cand[d, 2 * pair + parity, lead:lead + half, :] = rounded[at:at + half]
 
+    def send_last(d, t):
+        flag = (me // 2) % 2
+        oi = (sides - 1) * (1 - flag)
+        offset = oi - REACH + (oi + REACH) // (2 * REACH)
+
+        @pl.when(present(offset) & (t < frame_count - 1))
+        def _():
+            feature_copy(d, t, oi, sides - 1 - oi, offset).start()
+
     def finish(d, t):
         edge = margin * half
         for side in range(2):
@@ -512,9 +521,10 @@
                         axis=0,
                     ).astype(jnp.bfloat16)
 
-                @pl.when(present(offset))
-                def _():
-                    feature_copy(d, t, oi, sides - 1 - oi, offset).start()
+                if k < sides - 1:
+                    @pl.when(present(offset))
+                    def _():
+                        feature_copy(d, t, oi, sides - 1 - oi, offset).start()
 
         for side in range(2):
             @pl.when(present(1 if side else -1))
@@ -546,6 +556,7 @@
     def frame_step(t, carry):
         finish(0, t)
         inner(1)
+        send_last(0, t)
         finish(1, t)
 
         @pl.when(t == 0)
@@ -553,6 +564,7 @@
             lax.fori_loop(1, frame_count - 1, load_rest, 0)
 
         emit(t)
+        send_last(1, t)
 
         @pl.when(t < frame_count - 1)
         def _():

time: 40.2 us -> 40 us (level); the launches traced: 40.1 us -> 39.4 us
  Pallas kernels: 39.4 us -> 38.7 us
    pallas_call x1, Pallas kernels: 38.4 us -> 37.7 us  [on_device(): pl.pallas_call(functools.partial(sweep_kernel, dims), out_shape=(result,...]
where the time goes in v4:
time: 40 us; the launch traced here: 39.4 us
  Pallas kernels  38.7 us (97%)
  between operations  0.64 us (2%)
    pallas_call x1, Pallas kernels, on_device(): pl.pallas_call(functools.partial(sweep_kernel, dims), out_shape=(result,...  37.7 us
    pallas_call x1, Pallas kernels, on_device(): pl.pallas_call(store_kernel, out_shape=(plain, plain), in_specs=[pl.Block...  1.03 us

profile of v4, /device:TPU:11, one launch (start us, length us, event | category | flops | bytes accessed | tf_op | source)
XLA Modules:
  0.0 39.4 jit_solution(13177851982602015341)
XLA Ops:
  0.6 37.7 %shard_map.68 = (bf16[4,64,8,128]{3,2,1,0:T(8,128)(2,1)S(1)}, bf16[4,64,8,128]{3,2,1,0:T(8,128)(2,1)S(1)}) custom-call(bf16[4,64,8,128]{3,2,1,0:T(8,128)(2,1)} %frames_hbm.1, s32[3,16]{1,0:T(4,128)} %mf_hbm.1, s32[3,16]{1,0:T(4,128)} %mb_hbm.1, bf16[2,64,128]{2,1,0:T(8,128)(2,1)} %join_hbm.1, bf16[2,4,9,64,64]{4,3,2,1,0:T(8,128)(2,1)} %conv_ref.1), custom_call_target="tpu_custom_call" | custom-call | tf_op jit(solution)/shard_map/pallas_call | solution.py:613
  38.3 1.0 %shard_map.69 = (bf16[4,64,8,128]{3,2,1,0:T(8,128)(2,1)}, bf16[4,64,8,128]{3,2,1,0:T(8,128)(2,1)}) custom-call(bf16[4,64,8,128]{3,2,1,0:T(8,128)(2,1)S(1)} %get-tuple-element.4.ahead_ref, bf16[4,64,8,128]{3,2,1,0:T(8,128)(2,1)S(1)} %get-tuple-element.5.behind_ref), custom_call_target="tpu_custom_call" | custom-call | tf_op jit(solution)/shard_map/pallas_call | solution.py:653

commit v5 on v4

--- a/solution.py
+++ b/solution.py
@@ -27,6 +27,23 @@
     return lax.dot_general(
         left, right, (((1,), (1,)), ((), ())), preferred_element_type=jnp.float32
     )
+
+
+def planes(nat, flip, rows, cols):
+    lanes = nat.shape[2]
+    channels = lanes // 2
+    identity = (
+        lax.broadcasted_iota(jnp.int32, (lanes, lanes), 0)
+        == lax.broadcasted_iota(jnp.int32, (lanes, lanes), 1)
+    ).astype(jnp.bfloat16)
+    moved = [matmul_t(identity, nat[d].astype(jnp.bfloat16)) for d in range(2)]
+    for d in range(2):
+        for pair in range(rows // 2):
+            for low in range(2):
+                flip[d, pl.ds(2 * pair + low, channels, stride=rows), :] = moved[d][
+                    low * channels:(low + 1) * channels, pair * cols:(pair + 1) * cols
+                ]
+    return [flip[d].reshape(channels, rows, cols).astype(jnp.bfloat16) for d in range(2)]
 
 
 def sweep_kernel(
@@ -38,6 +55,7 @@
     conv_ref,
     ahead_ref,
     behind_ref,
+    nat,
     frames_ref,
     mf_ref,
     mb_ref,
@@ -45,7 +63,6 @@
     conv_v,
     x_ref,
     flip,
-    nat,
     wj_ref,
     wc_ref,
     mine,
@@ -207,26 +224,18 @@
         lax.fori_loop(0, layers, build_layer, 0)
 
     def emit(t):
-        identity = (
-            lax.broadcasted_iota(jnp.int32, (lanes, lanes), 0)
-            == lax.broadcasted_iota(jnp.int32, (lanes, lanes), 1)
-        ).astype(jnp.bfloat16)
         for d in range(2):
             for pair in range(own_pairs):
                 for parity in range(2):
                     nat[d, pl.ds(pair * cols + parity, half, stride=2), :] = cand[
                         d, 2 * pair + parity, lead:lead + half, :
                     ]
-        moved = [matmul_t(identity, nat[d].astype(jnp.bfloat16)) for d in range(2)]
-        for d in range(2):
-            for pair in range(own_pairs):
-                for low in range(2):
-                    flip[d, pl.ds(2 * pair + low, channels, stride=rows), :] = moved[d][
-                        low * channels:(low + 1) * channels, pair * cols:(pair + 1) * cols
-                    ]
-        for d in range(2):
-            now = t if d == 0 else frame_count - 1 - t
-            outs[d][now] = flip[d].reshape(channels, rows, cols).astype(jnp.bfloat16)
+
+        @pl.when(t < frame_count - 1)
+        def _():
+            for d, plane in enumerate(planes(nat, flip, rows, cols)):
+                now = t if d == 0 else frame_count - 1 - t
+                outs[d][now] = plane
 
     table_load = pltpu.make_async_copy(table_v, table_s, m_send.at[0])
 
@@ -509,7 +518,8 @@
             row = d * (frame_count - 1) + t
             flag = (me // 2) % 2
             for k in range(sides):
-                oi = k + flag * (sides - 1 - 2 * k)
+                order = (0, 2, 1, 3)[k]
+                oi = order + flag * (sides - 1 - 2 * order)
                 offset = oi - REACH + (oi + REACH) // (2 * REACH)
                 picks = [table_s[oi, row, bc + slot] for slot in range(cap)]
                 for tile in range(2 * own_pairs):
@@ -577,14 +587,24 @@
     lax.fori_loop(0, frame_count, frame_step, 0)
 
 
-def store_kernel(ahead_ref, behind_ref, ahead_out, behind_out, sems):
+def store_kernel(ahead_ref, behind_ref, nat, ahead_out, behind_out, flip, staged, sems):
+    frame_count, channels, rows, cols = ahead_out.shape
+    sources, targets = (ahead_ref, behind_ref), (ahead_out, behind_out)
+    last = (frame_count - 1, 0)
     copies = [
-        pltpu.make_async_copy(source.at[f], target.at[f], sems.at[k, f])
-        for k, (source, target) in enumerate([(ahead_ref, ahead_out), (behind_ref, behind_out)])
-        for f in range(source.shape[0])
+        pltpu.make_async_copy(sources[d].at[f], targets[d].at[f], sems.at[d, f])
+        for d in range(2)
+        for f in range(frame_count)
+        if f != last[d]
     ]
     for copy in copies:
         copy.start()
+    for d, plane in enumerate(planes(nat, flip, rows, cols)):
+        staged[d] = plane
+    for d in range(2):
+        copy = pltpu.make_async_copy(staged.at[d], targets[d].at[last[d]], sems.at[d, last[d]])
+        copy.start()
+        copies.append(copy)
     for copy in copies:
         copy.wait()
 
@@ -612,9 +632,9 @@
     edge = (2, margin * half, lanes)
     swept = pl.pallas_call(
         functools.partial(sweep_kernel, dims),
-        out_shape=(result, result),
+        out_shape=(result, result, pltpu.VMEM((2, own_pairs * cols, lanes), jnp.float32)),
         in_specs=[pl.BlockSpec(memory_space=pltpu.HBM)] * 5,
-        out_specs=(vmem, vmem),
+        out_specs=(vmem, vmem, vmem),
         scratch_shapes=[
             pltpu.VMEM(frames.shape, jnp.bfloat16),
             pltpu.VMEM(motion_forward.shape, jnp.int32),
@@ -623,7 +643,6 @@
             pltpu.VMEM(conv_weight.shape, jnp.bfloat16),
             pltpu.VMEM((frame_count, 2, own_pairs * half, lanes), jnp.bfloat16),
             pltpu.VMEM((2, channels * rows, cols), jnp.float32),
-            pltpu.VMEM((2, own_pairs * cols, lanes), jnp.float32),
             pltpu.VMEM((2, lanes, 2 * lanes), jnp.bfloat16),
             pltpu.VMEM((2, layers, 3, 2 * lanes, lanes), jnp.bfloat16),
             pltpu.VMEM((8, 128), jnp.int32),
@@ -653,9 +672,13 @@
     return pl.pallas_call(
         store_kernel,
         out_shape=(plain, plain),
-        in_specs=[pl.BlockSpec(memory_space=pl.ANY)] * 2,
+        in_specs=[pl.BlockSpec(memory_space=pl.ANY)] * 2 + [vmem],
         out_specs=(outside, outside),
-        scratch_shapes=[pltpu.SemaphoreType.DMA((2, frame_count))],
+        scratch_shapes=[
+            pltpu.VMEM((2, channels * rows, cols), jnp.float32),
+            pltpu.VMEM((2, channels, rows, cols), jnp.bfloat16),
+            pltpu.SemaphoreType.DMA((2, frame_count)),
+        ],
         compiler_params=pltpu.CompilerParams(vmem_limit_bytes=4 * 1024 * 1024),
     )(*swept)
 

time: 40 us -> 40.1 us (level)
  the two profiles are of different devices: /device:TPU:11 before, /device:TPU:3 now
where the time goes in v5:
time: 40.1 us; the launch traced here: 40 us
  Pallas kernels  39.3 us (98%)
  between operations  0.64 us (2%)
    pallas_call x1, Pallas kernels, on_device(): pl.pallas_call(functools.partial(sweep_kernel, dims), out_shape=(result,...  38.3 us
    pallas_call x1, Pallas kernels, on_device(): pl.pallas_call(store_kernel, out_shape=(plain, plain), in_specs=[pl.Block...  1.04 us

profile of v5, /device:TPU:3, one launch (start us, length us, event | category | flops | bytes accessed | tf_op | source)
XLA Modules:
  0.0 40.0 jit_solution(13361236353349946613)
XLA Ops:
  0.6 38.3 %shard_map.68 = (bf16[4,64,8,128]{3,2,1,0:T(8,128)(2,1)S(1)}, bf16[4,64,8,128]{3,2,1,0:T(8,128)(2,1)S(1)}, f32[2,512,128]{2,1,0:T(8,128)S(1)}) custom-call(bf16[4,64,8,128]{3,2,1,0:T(8,128)(2,1)} %frames_hbm.1, s32[3,16]{1,0:T(4,128)} %mf_hbm.1, s32[3,16]{1,0:T(4,128)} %mb_hbm.1, bf16[2,64,128]{2,1,0:T(8,128)(2,1)} %join_hbm.1, ...), custom_call_target="tpu_custom_call" | custom-call | tf_op jit(solution)/shard_map/pallas_call | solution.py:633
  38.9 1.0 %shard_map.69 = (bf16[4,64,8,128]{3,2,1,0:T(8,128)(2,1)}, bf16[4,64,8,128]{3,2,1,0:T(8,128)(2,1)}) custom-call(bf16[4,64,8,128]{3,2,1,0:T(8,128)(2,1)S(1)} %get-tuple-element.5.ahead_ref, bf16[4,64,8,128]{3,2,1,0:T(8,128)(2,1)S(1)} %get-tuple-element.6.behind_ref, f32[2,512,128]{2,1,0:T(8,128)S(1)} %get-tuple-element.7.nat), custom_call_target="tpu_custom_call" | custom-call | tf_op jit(solution)/shard_map/pallas_call | solution.py:672
